TPU v7x, 32 devices: a whole 2x2x4 slice. The times are simulated.
32 devices in a mesh: section: 4 (over y, x), dp: 4 (over z), mp: 2 (over core).
Axes of the slice: x: 2, y: 2, z: 4, core: 2. Of those that a mesh axis runs over, the one named last changes fastest.
Arguments:
- encoded: float32 [8, 64, 4096], P('dp', None, ('section', 'mp')), may hold values from -6 to 6
- counts: int32 [8], replicated, may hold values from 1 to 64, 384 in all
- owner: int32 [8], replicated, may hold values from 0 to 3, as said below
- w_key: bfloat16 [4, 4096, 2048], P('section', 'dp', 'mp'), may hold values from -0.09375 to 0.09375
- w_value: bfloat16 [4, 4096, 2048], P('section', 'dp', 'mp'), may hold values from -0.09375 to 0.09375
- queries: bfloat16 [4, 16, 128, 2048], P('section', 'dp', None, 'mp'), may hold values from -6 to 6
- grad_out: bfloat16 [4, 16, 128, 2048], P('section', 'dp', None, 'mp'), may hold values from -6 to 6
- dec_mask: int32 [16, 128], P('dp'), may hold values 0 or 1
Outputs:
- attn_out: bfloat16 [4, 16, 128, 2048], P('section', 'dp', None, 'mp')
- d_encoded: float32 [8, 64, 4096], P('dp', None, ('section', 'mp'))
Inputs may be any that keep to these rules, and one draw needn't show every extreme that they name: Each owner holds at most 4 dialogues and some owner holds exactly 4.
All inputs are finite; a program needn't handle non-finite values. No bound on the sum of `dec_mask` on one device may be relied on, other than what follows from the above.
Results may differ from a plain program's by a relative error of at most 0.014.
Values may be sent and summed in bfloat16 or wider, within the bound.
A program may use at most 128 MiB of HBM per device.

v0:
```python
import jax
import jax.numpy as jnp
from jax import lax
from jax.sharding import PartitionSpec as P

HEAD_DIM = 256


def attend(query_rows, key_rows, value_rows, grad_rows, slot_length, slot_live, answer_mask):
    slot_count, query_len, head_width = query_rows.shape
    key_len = key_rows.shape[1]
    head_count = head_width // HEAD_DIM
    score_scale = HEAD_DIM ** (-0.5)
    query_heads = query_rows.reshape(slot_count, query_len, head_count, HEAD_DIM)
    key_heads = key_rows.reshape(slot_count, key_len, head_count, HEAD_DIM)
    value_heads = value_rows.reshape(slot_count, key_len, head_count, HEAD_DIM)
    masked_grad = grad_rows * answer_mask.astype(jnp.bfloat16)[:, :, None]
    grad_heads = masked_grad.reshape(slot_count, query_len, head_count, HEAD_DIM)
    scores = (
        jnp.einsum("cqhd,ckhd->chqk", query_heads, key_heads, preferred_element_type=jnp.float32)
        * score_scale
    )
    inside = (
        jnp.arange(key_len, dtype=jnp.int32)[None, None, None, :] < slot_length[:, None, None, None]
    )
    unnormed = jnp.where(inside, jnp.exp(scores), 0.0)
    attention = unnormed / (
        jnp.sum(unnormed, axis=-1, keepdims=True) + (1.0 - slot_live)[:, None, None, None]
    )
    attn_probs = attention.astype(jnp.bfloat16)
    attended = jnp.einsum(
        "chqk,ckhd->cqhd", attn_probs, value_heads, preferred_element_type=jnp.float32
    ).astype(jnp.bfloat16)
    grad_values = jnp.einsum(
        "chqk,cqhd->ckhd", attn_probs, grad_heads, preferred_element_type=jnp.float32
    ).astype(jnp.bfloat16)
    grad_probs = jnp.einsum(
        "cqhd,ckhd->chqk", grad_heads, value_heads, preferred_element_type=jnp.float32
    )
    grad_scores = (
        attention * (grad_probs - jnp.sum(attention * grad_probs, axis=-1, keepdims=True))
    ).astype(jnp.bfloat16)
    grad_keys = (
        jnp.einsum("chqk,cqhd->ckhd", grad_scores, query_heads, preferred_element_type=jnp.float32)
        * score_scale
    ).astype(jnp.bfloat16)
    return (
        attended.reshape(slot_count, query_len, head_width),
        grad_keys.reshape(slot_count, key_len, head_width),
        grad_values.reshape(slot_count, key_len, head_width),
    )


def slot_table(owner, owner_index, capacity):
    dialog_ids = jnp.arange(owner.shape[0], dtype=jnp.int32)
    is_mine = (owner == owner_index).astype(jnp.int32)
    position = jnp.cumsum(is_mine) - 1
    picked = is_mine[None, :] * (
        position[None, :] == jnp.arange(capacity, dtype=jnp.int32)[:, None]
    ).astype(jnp.int32)
    slot_dialog = jnp.sum(picked * dialog_ids[None, :], axis=1)
    slot_valid = jnp.sum(picked, axis=1)
    return (slot_dialog, slot_valid)


def body(encoded, counts, owner, w_key, w_value, queries, grad_out, dec_mask):
    owner_index = lax.axis_index("dp")
    groups = lax.axis_size("dp")
    local_count = encoded.shape[0]
    dialog_count = owner.shape[0]
    capacity = queries.shape[1]
    encoded_bf = encoded.astype(jnp.bfloat16)
    slot_dialog, slot_valid = slot_table(owner, owner_index, capacity)
    slot_length = jnp.take(counts, slot_dialog) * slot_valid
    slot_live = slot_valid.astype(jnp.float32)
    slot_keep = slot_valid.astype(jnp.bfloat16)[:, None, None]
    own_ids = owner_index * local_count + jnp.arange(local_count, dtype=jnp.int32)
    target = jnp.take(owner, own_ids)
    routing = (target[None, :] == jnp.arange(groups, dtype=jnp.int32)[:, None])[:, :, None, None]
    key_w, value_w = (
        lax.all_gather(w_key[0], "dp", axis=0, tiled=True),
        lax.all_gather(w_value[0], "dp", axis=0, tiled=True),
    )
    model_width = key_w.shape[0]

    def project(row_block, weight):
        flat_rows = row_block.reshape(-1, model_width)
        product = jnp.dot(flat_rows, weight, preferred_element_type=jnp.float32).astype(
            jnp.bfloat16
        )
        return product.reshape(row_block.shape[0], row_block.shape[1], weight.shape[1])

    arrived = lax.all_to_all(
        jnp.where(routing, encoded_bf[None], 0), "dp", split_axis=0, concat_axis=0, tiled=True
    )
    flat_rows = arrived.reshape((dialog_count,) + arrived.shape[2:])
    gathered = lax.all_gather(
        jnp.take(flat_rows, slot_dialog, axis=0) * slot_keep, ("section", "mp"), axis=2, tiled=True
    )
    slot_keys = project(gathered, key_w)
    slot_values = project(gathered, value_w)
    attended, grad_keys, grad_values = attend(
        queries[0], slot_keys, slot_values, grad_out[0], slot_length, slot_live, dec_mask
    )
    row_count, key_len, head_width = grad_keys.shape
    numbers = (((1,), (1,)), ((), ()))
    layer_terms = lax.dot_general(
        grad_keys.reshape(-1, head_width), key_w, numbers, preferred_element_type=jnp.float32
    )
    layer_terms = layer_terms + lax.dot_general(
        grad_values.reshape(-1, head_width), value_w, numbers, preferred_element_type=jnp.float32
    )
    layer_terms = layer_terms.reshape(row_count, key_len, model_width)
    summed = lax.psum_scatter(
        layer_terms.astype(jnp.bfloat16), ("section", "mp"), scatter_dimension=2, tiled=True
    ).astype(jnp.float32)
    placed = jnp.zeros((dialog_count,) + summed.shape[1:], summed.dtype)
    placed = placed.at[slot_dialog].add(summed * slot_keep.astype(summed.dtype))
    returned = lax.all_to_all(
        placed.reshape((groups, local_count) + summed.shape[1:]).astype(jnp.bfloat16),
        "dp",
        split_axis=0,
        concat_axis=0,
        tiled=True,
    ).astype(jnp.float32)
    d_encoded = jnp.sum(returned, axis=0)
    return (attended[None], d_encoded)


def solution(mesh):
    placed = (
        P("dp", None, ("section", "mp")),
        P(),
        P(),
        P("section", "dp", "mp"),
        P("section", "dp", "mp"),
        P("section", "dp", None, "mp"),
        P("section", "dp", None, "mp"),
        P("dp", None),
    )
    return jax.shard_map(
        body,
        mesh=mesh,
        in_specs=placed,
        out_specs=(P("section", "dp", None, "mp"), P("dp", None, ("section", "mp"))),
        check_vma=False,
    )
```

profile of v0, /device:TPU:25, one launch (start us, length us, event | category | flops | bytes accessed | tf_op | source)
XLA Modules:
  0.0 447.6 jit_solution(7574430008458336703)
XLA Ops:
  7.2 1.3 gather_fusion
  8.5 1.1 convert_element_type.86
  9.6 0.9 broadcast_select_fusion
  10.5 4.5 %all-to-all-start = ((bf16[4,2,64,512]{3,2,1,0:T(8,128)(2,1)}), bf16[4,2,64,512]{3,2,1,0:T(8,128)(2,1)S(1)}, u32[]{:S(2)}, u32[]{:S(2)}) async-start(bf16[4,2,64,512]{3,2,1,0:T(8,128)(2,1)} %broadcast_select_fusion), calls=%async_computation | async-start | bytes 1048576 | tf_op jit(solution)/shard_map/all_to_all | solution.py:93
  17.5 8.8 %all-to-all-done = bf16[4,2,64,512]{3,2,1,0:T(8,128)(2,1)S(1)} async-done(((bf16[4,2,64,512]{3,2,1,0:T(8,128)(2,1)}), bf16[4,2,64,512]{3,2,1,0:T(8,128)(2,1)S(1)}, u32[]{:S(2)}, u32[]{:S(2)}) %all-to-all-start) | async-done | bytes 524320 | tf_op jit(solution)/shard_map/all_to_all | solution.py:93
  26.9 0.8 select_multiply_fusion
  29.3 1.6 reshape_squeeze.3
  30.8 1.6 squeeze.11
  32.5 26.3 %all-gather.6.cloned.1.call-done = bf16[4,64,4096]{2,1,0:T(8,128)(2,1)} async-done(((bf16[4,64,512]{2,1,0:T(8,128)(2,1)}), bf16[4,64,4096]{2,1,0:T(8,128)(2,1)}) %all-gather.6.cloned.1.call-update) | async-done | bytes 2097168 | tf_op jit(solution)/shard_map/all_gather | solution.py:97
  58.8 147.9 %all-gather.8.cloned.1.call-done = bf16[1,4096,1024]{2,1,0:T(8,128)(2,1)} async-done(((bf16[1,1024,1024]{2,1,0:T(8,128)(2,1)}), bf16[1,4096,1024]{2,1,0:T(8,128)(2,1)}) %all-gather.8.cloned.1.call-update) | async-done | bytes 8388624 | tf_op jit(solution)/shard_map/all_gather | solution.py:82
  206.7 6.3 %fusion.14 = bf16[256,1024]{1,0:T(8,128)(2,1)S(1)} fusion(bf16[256,4096]{1,0:T(8,128)(2,1)} %bitcast.66, bf16[1,4096,1024]{2,1,0:T(8,128)(2,1)} %all-gather.8.cloned.1.call-done), kind=kOutput, calls=%fused_computation.16 | convolution fusion | flops 2147745792 | bytes 11010048 | tf_op jit(solution)/shard_map/dot_general | solution.py:88
  213.5 142.7 %all-gather.10.cloned.1.call-done = bf16[1,4096,1024]{2,1,0:T(8,128)(2,1)} async-done(((bf16[1,1024,1024]{2,1,0:T(8,128)(2,1)}), bf16[1,4096,1024]{2,1,0:T(8,128)(2,1)}) %all-gather.10.cloned.1.call-update) | async-done | bytes 8388624 | tf_op jit(solution)/shard_map/all_gather | solution.py:81
  356.1 7.2 %fusion.17 = bf16[256,1024]{1,0:T(8,128)(2,1)} fusion(bf16[256,4096]{1,0:T(8,128)(2,1)} %bitcast.67, bf16[1,4096,1024]{2,1,0:T(8,128)(2,1)} %all-gather.10.cloned.1.call-done), kind=kOutput, calls=%fused_computation.17 | convolution fusion | flops 2147745792 | bytes 11010048 | tf_op jit(solution)/shard_map/dot_general | solution.py:88
  363.3 1.4 reshape_reshape.13
  367.8 1.2 slice-done.3
  369.0 4.3 fusion
  373.4 6.0 %fusion.11 = bf16[256,4096]{1,0:T(8,128)(2,1)} fusion(f32[256,4096]{1,0:T(8,128)} %fusion, bf16[256,1024]{1,0:T(8,128)(2,1)S(1)} %bitcast.61, bf16[1,4096,1024]{2,1,0:T(8,128)(2,1)S(1)} %bitcast.63), kind=kOutput, calls=%fused_computation.13 | convolution fusion | flops 2149580800 | bytes 15204352 | tf_op jit(solution)/shard_map/dot_general | solution.py:110
  379.4 42.2 %reduce-scatter.2.cloned.1.call-done = bf16[4,64,512]{2,1,0:T(8,128)(2,1)} async-done(((bf16[4,64,4096]{2,1,0:T(8,128)(2,1)}), bf16[4,64,512]{2,1,0:T(8,128)(2,1)}) %reduce-scatter.2.cloned.1.call-update) | async-done | bytes 262160 | tf_op jit(solution)/shard_map/reduce_scatter | solution.py:114
  421.6 1.1 convert_multiply_fusion
  422.8 0.9 scatter_fusion
  423.7 0.9 convert_element_type.104
  424.5 4.5 %all-to-all-start.1 = ((bf16[4,2,64,512]{3,2,1,0:T(8,128)(2,1)}), bf16[4,2,64,512]{3,2,1,0:T(8,128)(2,1)S(1)}, u32[]{:S(2)}, u32[]{:S(2)}) async-start(bf16[4,2,64,512]{3,2,1,0:T(8,128)(2,1)} %bitcast.15), calls=%async_computation.2 | async-start | bytes 1048576 | tf_op jit(solution)/shard_map/all_to_all | solution.py:119
  429.6 1.3 copy.34
  430.9 9.5 %all-to-all-done.1 = bf16[4,2,64,512]{3,2,1,0:T(8,128)(2,1)S(1)} async-done(((bf16[4,2,64,512]{3,2,1,0:T(8,128)(2,1)}), bf16[4,2,64,512]{3,2,1,0:T(8,128)(2,1)S(1)}, u32[]{:S(2)}, u32[]{:S(2)}) %all-to-all-start.1) | async-done | bytes 524320 | tf_op jit(solution)/shard_map/all_to_all | solution.py:119
  (63 shorter events, 9.3 us)
Async XLA Ops:
  7.2 9.6 %copy-start = (s32[8]{0:T(128)S(1)}, s32[8]{0:T(128)}, u32[]{:S(2)}) copy-start(s32[8]{0:T(128)} %param.9) | copy-start | bytes 100
  8.5 20.7 %copy-start.5 = (s32[4,128]{1,0:T(4,128)S(1)}, s32[4,128]{1,0:T(4,128)}, u32[]{:S(2)}) copy-start(s32[4,128]{1,0:T(4,128)} %param.15) | copy-start | bytes 6148
  8.5 20.7 %copy-start.1 = (bf16[1,4,128,1024]{3,2,1,0:T(8,128)(2,1)S(1)}, bf16[1,4,128,1024]{3,2,1,0:T(8,128)(2,1)}, u32[]{:S(2)}) copy-start(bf16[1,4,128,1024]{3,2,1,0:T(8,128)(2,1)} %param.13) | copy-start | bytes 3145732
  10.5 15.8 %all-to-all-start = ((bf16[4,2,64,512]{3,2,1,0:T(8,128)(2,1)}), bf16[4,2,64,512]{3,2,1,0:T(8,128)(2,1)S(1)}, u32[]{:S(2)}, u32[]{:S(2)}) async-start(bf16[4,2,64,512]{3,2,1,0:T(8,128)(2,1)} %broadcast_select_fusion), calls=%async_computation | async-start | bytes 1048576 | tf_op jit(solution)/shard_map/all_to_all | solution.py:93
  15.0 15.8 %copy-start.2 = (bf16[1,4,128,1024]{3,2,1,0:T(8,128)(2,1)S(1)}, bf16[1,4,128,1024]{3,2,1,0:T(8,128)(2,1)}, u32[]{:S(2)}) copy-start(bf16[1,4,128,1024]{3,2,1,0:T(8,128)(2,1)} %param.14) | copy-start | bytes 3145732
  15.0 43.8 %all-gather.6.cloned.1.call-start = ((), (), s32[]{:S(2)}) async-start(), calls=%async_computation.3 | async-start | bytes 2359296 | tf_op jit(solution)/shard_map/all_gather | solution.py:97
  27.7 179.0 %all-gather.8.cloned.1.call-start = ((), (), s32[]{:S(2)}) async-start(), calls=%async_computation.5 | async-start | bytes 10485760 | tf_op jit(solution)/shard_map/all_gather | solution.py:82
  28.4 327.7 %all-gather.10.cloned.1.call-start = ((), (), s32[]{:S(2)}) async-start(), calls=%async_computation.6 | async-start | bytes 10485760 | tf_op jit(solution)/shard_map/all_gather | solution.py:81
  29.2 392.4 %reduce-scatter.2.cloned.1.call-start = ((), (), s32[]{:S(2)}) async-start(), calls=%async_computation.4 | async-start | bytes 2359296 | tf_op jit(solution)/shard_map/reduce_scatter | solution.py:114
  213.5 151.3 %copy-start.3 = (bf16[4,128,4,256]{3,2,1,0:T(4,128)(2,1)S(1)}, bf16[4,128,4,256]{3,2,1,0:T(4,128)(2,1)}, u32[]{:S(2)}) copy-start(bf16[4,128,4,256]{3,2,1,0:T(4,128)(2,1)} %reshape_squeeze.3) | copy-start | bytes 3145732
  213.5 151.9 %copy-start.4 = (bf16[4,128,4,256]{3,2,1,0:T(4,128)(2,1)S(1)}, bf16[4,128,4,256]{3,2,1,0:T(4,128)(2,1)}, u32[]{:S(2)}) copy-start(bf16[4,128,4,256]{3,2,1,0:T(4,128)(2,1)} %squeeze.11) | copy-start | bytes 3145732
  365.3 1.1 copy-start.6
  365.4 2.4 slice-start.2
  365.8 3.2 slice-start.3
  367.7 5.7 %slice-start = ((s8[8388608]{0:T(1024)(128)(4,1)}), s8[4194304]{0:T(1024)(128)(4,1)S(1)}, s32[]{:S(2)}) async-start(s8[8388608]{0:T(1024)(128)(4,1)} %bitcast.62), calls=%async_computation.7 | async-start | bytes 8388608
  369.0 4.3 slice-start.1
  379.4 49.7 %copy-start.7 = (f32[4,4,128,64]{2,3,1,0:T(8,128)S(1)}, f32[4,4,128,64]{2,3,1,0:T(8,128)}, u32[]{:S(2)}) copy-start(f32[4,4,128,64]{2,3,1,0:T(8,128)} %copy-done.6) | copy-start | bytes 1572868
  424.5 15.8 %all-to-all-start.1 = ((bf16[4,2,64,512]{3,2,1,0:T(8,128)(2,1)}), bf16[4,2,64,512]{3,2,1,0:T(8,128)(2,1)S(1)}, u32[]{:S(2)}, u32[]{:S(2)}) async-start(bf16[4,2,64,512]{3,2,1,0:T(8,128)(2,1)} %bitcast.15), calls=%async_computation.2 | async-start | bytes 1048576 | tf_op jit(solution)/shard_map/all_to_all | solution.py:119
Sparse Core Ops, SparseCore 0:
  27.8 30.9 all-gather.5
  60.4 146.3 all-gather.7
  208.3 147.7 all-gather.9
  379.5 42.0 reduce-scatter.1
where the time goes:
time: 453 us; the launch traced here: 448 us
  waiting for transfers between devices  379 us (84%)
  matrix products  26.2 us (6%)
  between operations  14 us (3%)
  local copies, waits for them, and re-layouts  11.2 us (2%)
  starting transfers between devices  9.18 us (2%)
  other arithmetic  8.3 us (2%)
    all_gather x1, waiting for transfers between devices, body(): lax.all_gather(w_value[0], 'dp', axis=0, tiled=True)  148 us
    all_gather x1, waiting for transfers between devices, body(): lax.all_gather(w_key[0], 'dp', axis=0, tiled=True)  143 us
    reduce_scatter x1, waiting for transfers between devices, body(): lax.psum_scatter(layer_terms.astype(jnp.bfloat16), ('section', 'mp'), sca...  42.2 us
    all_gather x1, waiting for transfers between devices, body(): lax.all_gather(jnp.take(flat_rows, slot_dialog, axis=0) * slot_keep, ('se...  26.3 us
    dot_general x2, matrix products, project(): jnp.dot(flat_rows, weight, preferred_element_type=jnp.float32)  13.5 us
    all_to_all x1, waiting for transfers between devices, body(): lax.all_to_all(placed.reshape((groups, local_count) + summed.shape[1:]).a...  9.47 us
  transfers between devices with their start and end apart: 6, of which 6 were waited for; matrix products, arithmetic and copies ran while one was open for 3% of the time, Pallas kernels for 0%

commit v1 on v0

v1 whole, which is shorter than its diff:
```python
import functools

import jax
import jax.numpy as jnp
from jax import lax
from jax.experimental import pallas as pl
from jax.experimental.pallas import tpu as pltpu
from jax.sharding import PartitionSpec as P

HEAD_DIM = 256
MESH = pl.DeviceIdType.MESH
SUB = 2
F32 = jnp.float32
BF16 = jnp.bfloat16


def dot(left, right, left_dim, right_dim):
    return lax.dot_general(
        left, right, (((left_dim,), (right_dim,)), ((), ())), preferred_element_type=F32
    )


def kernel(
    dims,
    counts,
    owner,
    encoded,
    w_key,
    w_value,
    queries,
    grad_out,
    mask,
    attn_out,
    d_encoded,
    table,
    weights,
    enc_cast,
    enc_all,
    part,
    fwd_recv,
    fwd_send,
    own_grad,
    bwd_recv,
    bwd_send,
    acc,
    d_send,
    d_recv,
    d_fin,
    d_arrived,
    w_sem,
    swap_send,
    swap_recv,
    self_sem,
    enc_send_sem,
    enc_recv_sem,
    fwd_send_sem,
    fwd_recv_sem,
    bwd_send_sem,
    bwd_recv_sem,
    d_send_sem,
    d_recv_sem,
):
    sections, groups, cores = dims
    section = lax.axis_index("section")
    p = lax.axis_index("dp")
    core = lax.axis_index("mp")
    fold = sections // groups
    plane = sections * cores
    me = section * cores + core
    local_count, key_len, feat = encoded.shape
    dialogs = local_count * groups
    block_rows = local_count * key_len
    cap = queries.shape[0]
    heads = queries.shape[2] // HEAD_DIM
    per = dialogs // SUB
    pieces = 2 * heads * SUB
    scale = HEAD_DIM ** (-0.5)

    to_section, to_p = p * fold + lax.rem(section, fold), section // fold
    from_section, from_p = p * fold + lax.rem(section, fold), section // fold
    stays = section // fold == p

    def region(index):
        s, m = index // cores, lax.rem(index, cores)
        rows = pl.multiple_of((s // fold) * block_rows, block_rows)
        cols = pl.multiple_of((lax.rem(s, fold) * cores + m) * feat, feat)
        return pl.ds(rows, block_rows), pl.ds(cols, feat)

    copies = []
    for h in range(heads):
        for kv, ref in enumerate((w_key, w_value)):
            copy = pltpu.make_async_copy(
                ref.at[:, pl.ds(h * HEAD_DIM, HEAD_DIM)],
                weights.at[2 * h + kv],
                w_sem.at[2 * h + kv],
            )
            copy.start()
            copies.append(copy)

    barrier = pltpu.get_barrier_semaphore()

    def greet(s, z, m):
        pl.semaphore_signal(barrier, inc=1, device_id=(s, z, m), device_id_type=MESH)

    @pl.when(jnp.logical_not(stays))
    def _():
        greet(to_section, to_p, core)

    @pl.when(p > 0)
    def _():
        greet(section, p - 1, core)

    @pl.when(p < groups - 1)
    def _():
        greet(section, p + 1, core)

    @pl.loop(1, plane)
    def _(i):
        peer = lax.rem(me + i, plane)
        greet(peer // cores, p, lax.rem(peer, cores))

    for a in range(local_count):
        enc_cast[pl.ds(a * key_len, key_len), :] = encoded[a].astype(BF16)

    taken = jnp.int32(0)
    slot_dialog = [jnp.int32(0)] * cap
    slot_valid = [jnp.int32(0)] * cap
    slot_length = [jnp.int32(0)] * cap
    for d in range(dialogs):
        mine = (owner[d] == p).astype(jnp.int32)
        table[3 * cap + d] = jnp.where(mine == 1, jnp.minimum(taken, cap), cap)
        for c in range(cap):
            hit = mine * (taken == c).astype(jnp.int32)
            slot_dialog[c] = slot_dialog[c] + hit * d
            slot_valid[c] = slot_valid[c] + hit
            slot_length[c] = slot_length[c] + hit * counts[d]
        taken = taken + mine
    for c in range(cap):
        table[c] = slot_dialog[c]
        table[cap + c] = slot_valid[c]
        table[2 * cap + c] = slot_length[c]

    acc[...] = jnp.zeros_like(acc)
    own_grad[:, cap] = jnp.zeros((own_grad.shape[0],) + own_grad.shape[2:], BF16)

    pl.semaphore_wait(
        barrier,
        plane
        - 1
        + jnp.where(stays, 0, 1)
        + jnp.where(p > 0, 1, 0)
        + jnp.where(p < groups - 1, 1, 0),
    )

    target = to_section * cores + core
    t_rows, t_cols = region(target)
    m_rows, m_cols = region(me)

    def swap_copy():
        return pltpu.make_async_remote_copy(
            src_ref=enc_cast,
            dst_ref=enc_all.at[t_rows, t_cols],
            send_sem=swap_send.at[0],
            recv_sem=swap_recv.at[0],
            device_id=(to_section, to_p, core),
            device_id_type=MESH,
        )

    @pl.when(stays)
    def _():
        copy = pltpu.make_async_copy(enc_cast, enc_all.at[m_rows, m_cols], self_sem.at[0])
        copy.start()
        copy.wait()

    @pl.when(jnp.logical_not(stays))
    def _():
        swap_copy().start()
        pltpu.make_async_remote_copy(
            src_ref=enc_cast,
            dst_ref=enc_all.at[m_rows, m_cols],
            send_sem=swap_send.at[0],
            recv_sem=swap_recv.at[0],
            device_id=(from_section, from_p, core),
            device_id_type=MESH,
        ).wait_recv()

    def plane_copy(peer):
        return pltpu.make_async_remote_copy(
            src_ref=enc_all.at[m_rows, m_cols],
            dst_ref=enc_all.at[m_rows, m_cols],
            send_sem=enc_send_sem.at[peer],
            recv_sem=enc_recv_sem.at[me],
            device_id=(peer // cores, p, lax.rem(peer, cores)),
            device_id_type=MESH,
        )

    def plane_arrival(peer):
        rows, cols = region(peer)
        return pltpu.make_async_remote_copy(
            src_ref=enc_all.at[rows, cols],
            dst_ref=enc_all.at[rows, cols],
            send_sem=enc_send_sem.at[peer],
            recv_sem=enc_recv_sem.at[peer],
            device_id=(peer // cores, p, lax.rem(peer, cores)),
            device_id_type=MESH,
        )

    @pl.loop(1, plane)
    def _(i):
        plane_copy(lax.rem(me + i, plane)).start()

    for copy in copies:
        copy.wait()

    @pl.loop(1, plane)
    def _(i):
        plane_arrival(lax.rem(me + plane - i, plane)).wait_recv()

    def hop(recv, send, send_sem, recv_sem, way, j):
        other = p + 1 if way == 0 else p - 1
        return pltpu.make_async_remote_copy(
            src_ref=send.at[way, j],
            dst_ref=recv.at[way, j],
            send_sem=send_sem.at[way, j],
            recv_sem=recv_sem.at[way, j],
            device_id=(section, other, core),
            device_id_type=MESH,
        )

    def is_first(way):
        return p == 0 if way == 0 else p == groups - 1

    def is_last(way):
        return p == groups - 1 if way == 0 else p == 0

    fwd_hop = functools.partial(hop, fwd_recv, fwd_send, fwd_send_sem, fwd_recv_sem)
    bwd_hop = functools.partial(hop, bwd_recv, bwd_send, bwd_send_sem, bwd_recv_sem)

    def own_rows(j):
        sub = lax.rem(j, SUB)
        return [own_grad[j // SUB, table[3 * cap + sub * per + i]] for i in range(per)]

    def far(way):
        return p if way == 0 else groups - 1 - p

    def inside(j):
        return jnp.logical_and(j >= 0, j < pieces)

    def project(j):
        rows = pl.multiple_of(lax.rem(j, SUB) * (per * key_len), per * key_len)
        product = dot(enc_all[pl.ds(rows, per * key_len), :], weights[j // SUB], 1, 0)
        part[j] = product.astype(BF16).reshape(per, key_len, HEAD_DIM)

    def attend(h):
        cols = pl.ds(pl.multiple_of(h * HEAD_DIM, HEAD_DIM), HEAD_DIM)
        for c in range(cap):
            d = table[c]
            live = table[cap + c]
            length = table[2 * cap + c]
            keep = live.astype(F32)
            keys = (part[2 * h * SUB + d // per, lax.rem(d, per)].astype(F32) * keep).astype(BF16)
            values = (
                part[(2 * h + 1) * SUB + d // per, lax.rem(d, per)].astype(F32) * keep
            ).astype(BF16)
            q = queries[c, :, cols]
            g = (grad_out[c, :, cols].astype(F32) * mask[c]).astype(BF16)
            scores = dot(q, keys, 1, 1) * scale
            ok = lax.broadcasted_iota(jnp.int32, scores.shape, 1) < length
            unnormed = jnp.where(ok, jnp.exp(scores), 0.0)
            attention = unnormed / (jnp.sum(unnormed, axis=1, keepdims=True) + (1.0 - keep))
            probs = attention.astype(BF16)
            attn_out[c, :, cols] = dot(probs, values, 1, 0).astype(BF16)
            own_grad[2 * h + 1, c] = dot(probs, g, 0, 0).astype(BF16)
            grad_probs = dot(g, values, 1, 1)
            grad_scores = (
                attention
                * (grad_probs - jnp.sum(attention * grad_probs, axis=1, keepdims=True))
            ).astype(BF16)
            own_grad[2 * h, c] = (dot(grad_scores, q, 0, 0) * scale).astype(BF16)

    ready = 2 * SUB - 1 + groups - 1
    steps = pieces + ready + groups

    @pl.loop(0, steps)
    def _(t):
        @pl.when(t < pieces)
        def _():
            project(t)

        for way in range(2):
            j = t - far(way)

            @pl.when(inside(j))
            def _(way=way, j=j):
                @pl.when(is_first(way))
                def _():
                    fwd_send[way, j] = part[j]

                @pl.when(jnp.logical_not(is_first(way)))
                def _():
                    fwd_hop(way, j).wait_recv()

                @pl.when(jnp.logical_not(jnp.logical_or(is_first(way), is_last(way))))
                def _():
                    fwd_send[way, j] = (
                        part[j].astype(F32) + fwd_recv[way, j].astype(F32)
                    ).astype(BF16)

                @pl.when(jnp.logical_not(is_last(way)))
                def _():
                    fwd_hop(way, j).start()

        whole = t - (groups - 1)

        @pl.when(inside(whole))
        def _():
            @pl.when(p == 0)
            def _():
                part[whole] = (
                    part[whole].astype(F32) + fwd_recv[1, whole].astype(F32)
                ).astype(BF16)

            @pl.when(p == groups - 1)
            def _():
                part[whole] = (
                    part[whole].astype(F32) + fwd_recv[0, whole].astype(F32)
                ).astype(BF16)

            @pl.when(jnp.logical_and(p > 0, p < groups - 1))
            def _():
                part[whole] = (
                    part[whole].astype(F32)
                    + fwd_recv[0, whole].astype(F32)
                    + fwd_recv[1, whole].astype(F32)
                ).astype(BF16)

            @pl.when(lax.rem(whole, 2 * SUB) == 2 * SUB - 1)
            def _():
                attend(whole // (2 * SUB))

        for way in range(2):
            j = t - ready - far(way)

            @pl.when(inside(j))
            def _(way=way, j=j):
                @pl.when(is_first(way))
                def _():
                    for i, rows in enumerate(own_rows(j)):
                        bwd_send[way, j, i] = rows

                @pl.when(jnp.logical_not(is_first(way)))
                def _():
                    bwd_hop(way, j).wait_recv()

                @pl.when(jnp.logical_not(jnp.logical_or(is_first(way), is_last(way))))
                def _():
                    for i, rows in enumerate(own_rows(j)):
                        bwd_send[way, j, i] = rows + bwd_recv[way, j, i]

                @pl.when(jnp.logical_not(is_last(way)))
                def _():
                    bwd_hop(way, j).start()

        done = t - ready - (groups - 1)

        @pl.when(inside(done))
        def _():
            base = pl.multiple_of(lax.rem(done, SUB) * (per * key_len), per * key_len)

            @pl.when(p == 0)
            def _():
                for i, rows in enumerate(own_rows(done)):
                    part[done, i] = rows + bwd_recv[1, done, i]

            @pl.when(p == groups - 1)
            def _():
                for i, rows in enumerate(own_rows(done)):
                    part[done, i] = rows + bwd_recv[0, done, i]

            @pl.when(jnp.logical_and(p > 0, p < groups - 1))
            def _():
                for i, rows in enumerate(own_rows(done)):
                    part[done, i] = rows + bwd_recv[0, done, i] + bwd_recv[1, done, i]

            grads = part[done].reshape(per * key_len, HEAD_DIM)
            acc[pl.ds(base, per * key_len), :] += dot(grads, weights[done // SUB], 1, 1)

    @pl.loop(0, pieces)
    def _(j):
        for way in range(2):

            @pl.when(jnp.logical_not(is_last(way)))
            def _(way=way):
                fwd_hop(way, j).wait_send()
                bwd_hop(way, j).wait_send()

    d_send[...] = acc[...].astype(BF16)

    def term_copy(peer):
        rows, cols = region(peer)
        return pltpu.make_async_remote_copy(
            src_ref=d_send.at[rows, cols],
            dst_ref=d_recv.at[me],
            send_sem=d_send_sem.at[peer],
            recv_sem=d_recv_sem.at[me],
            device_id=(peer // cores, p, lax.rem(peer, cores)),
            device_id_type=MESH,
        )

    def term_arrival(peer):
        rows, cols = region(peer)
        return pltpu.make_async_remote_copy(
            src_ref=d_send.at[rows, cols],
            dst_ref=d_recv.at[peer],
            send_sem=d_send_sem.at[peer],
            recv_sem=d_recv_sem.at[peer],
            device_id=(peer // cores, p, lax.rem(peer, cores)),
            device_id_type=MESH,
        )

    @pl.loop(1, plane)
    def _(i):
        term_copy(lax.rem(me + i, plane)).start()

    total = acc.at[m_rows, m_cols]

    @pl.loop(1, plane)
    def _(i):
        peer = lax.rem(me + plane - i, plane)
        term_arrival(peer).wait_recv()
        total[...] += d_recv[peer].astype(F32)

    d_fin[...] = total[...].astype(BF16)

    def back_copy():
        return pltpu.make_async_remote_copy(
            src_ref=d_fin,
            dst_ref=d_arrived,
            send_sem=swap_send.at[1],
            recv_sem=swap_recv.at[1],
            device_id=(from_section, from_p, core),
            device_id_type=MESH,
        )

    @pl.when(stays)
    def _():
        for a in range(local_count):
            d_encoded[a] = d_fin[pl.ds(a * key_len, key_len), :].astype(F32)

    @pl.when(jnp.logical_not(stays))
    def _():
        back_copy().start()
        back_copy().wait_recv()
        for a in range(local_count):
            d_encoded[a] = d_arrived[pl.ds(a * key_len, key_len), :].astype(F32)

    @pl.loop(1, plane)
    def _(i):
        peer = lax.rem(me + i, plane)
        plane_copy(peer).wait_send()
        term_copy(peer).wait_send()

    @pl.when(jnp.logical_not(stays))
    def _():
        swap_copy().wait_send()
        back_copy().wait_send()


def body(dims, encoded, counts, owner, w_key, w_value, queries, grad_out, dec_mask):
    sections, groups, cores = dims
    local_count, key_len, feat = encoded.shape
    dialogs = local_count * groups
    cap, query_len, width = queries.shape[1:]
    model_rows = w_key.shape[1]
    heads = width // HEAD_DIM
    per = dialogs // SUB
    pieces = 2 * heads * SUB
    plane = sections * cores
    block_rows = local_count * key_len
    stream = pltpu.VMEM((2, pieces, per, key_len, HEAD_DIM), BF16)
    dma = pltpu.SemaphoreType.DMA
    vmem = pl.BlockSpec(memory_space=pltpu.VMEM)
    smem = pl.BlockSpec(memory_space=pltpu.SMEM)
    hbm = pl.BlockSpec(memory_space=pl.ANY)
    mask = dec_mask.astype(F32)[:, :, None]
    attended, d_encoded = pl.pallas_call(
        functools.partial(kernel, dims),
        out_shape=(
            jax.ShapeDtypeStruct((cap, query_len, width), BF16),
            jax.ShapeDtypeStruct((local_count, key_len, feat), F32),
        ),
        in_specs=[smem, smem, vmem, hbm, hbm, vmem, vmem, vmem],
        out_specs=(vmem, vmem),
        scratch_shapes=[
            pltpu.SMEM((3 * cap + dialogs,), jnp.int32),
            pltpu.VMEM((2 * heads, model_rows, HEAD_DIM), BF16),
            pltpu.VMEM((block_rows, feat), BF16),
            pltpu.VMEM((dialogs * key_len, model_rows), BF16),
            pltpu.VMEM((pieces, per, key_len, HEAD_DIM), BF16),
            stream,
            stream,
            pltpu.VMEM((2 * heads, cap + 1, key_len, HEAD_DIM), BF16),
            stream,
            stream,
            pltpu.VMEM((dialogs * key_len, model_rows), F32),
            pltpu.VMEM((dialogs * key_len, model_rows), BF16),
            pltpu.VMEM((plane, block_rows, feat), BF16),
            pltpu.VMEM((block_rows, feat), BF16),
            pltpu.VMEM((block_rows, feat), BF16),
            dma((2 * heads,)),
            dma((2,)),
            dma((2,)),
            dma((1,)),
            dma((plane,)),
            dma((plane,)),
            dma((2, pieces)),
            dma((2, pieces)),
            dma((2, pieces)),
            dma((2, pieces)),
            dma((plane,)),
            dma((plane,)),
        ],
        compiler_params=pltpu.CompilerParams(
            collective_id=0, has_side_effects=True, vmem_limit_bytes=60 * 1024 * 1024
        ),
    )(counts, owner, encoded, w_key[0], w_value[0], queries[0], grad_out[0], mask)
    return (attended[None], d_encoded)


def solution(mesh):
    placed = (
        P("dp", None, ("section", "mp")),
        P(),
        P(),
        P("section", "dp", "mp"),
        P("section", "dp", "mp"),
        P("section", "dp", None, "mp"),
        P("section", "dp", None, "mp"),
        P("dp", None),
    )
    dims = tuple(mesh.shape[name] for name in ("section", "dp", "mp"))
    return jax.shard_map(
        functools.partial(body, dims),
        mesh=mesh,
        in_specs=placed,
        out_specs=(P("section", "dp", None, "mp"), P("dp", None, ("section", "mp"))),
        check_vma=False,
    )
```

time: 453 us -> 173 us (0.38); the launches traced: 448 us -> 173 us
  waiting for transfers between devices: 379 us -> 0 us
  Pallas kernels: 0 us -> 168 us
  matrix products: 26.2 us -> 0 us
  between operations: 14 us -> 0.65 us
  starting transfers between devices: 9.18 us -> 0 us
  other arithmetic: 8.3 us -> 0.68 us
  local copies, waits for them, and re-layouts: 11.2 us -> 3.87 us
    all_gather x3 -> x0, waiting for transfers between devices: 317 us -> none  [the longest x1 148 us: body(): lax.all_gather(w_value[0], 'dp', axis=0, tiled=True)]
    pallas_call x0 -> x1, Pallas kernels: none -> 168 us  [body(): pl.pallas_call(functools.partial(kernel, dims), out_shape=(jax.ShapeDtype...]
    reduce_scatter x1 -> x0, waiting for transfers between devices: 42.2 us -> none  [body(): lax.psum_scatter(layer_terms.astype(jnp.bfloat16), ('section', 'mp'), sca...]
    dot_general x9 -> x0, matrix products: 26.2 us -> none  [the longest x2 13.5 us: project(): jnp.dot(flat_rows, weight, preferred_element_type=jnp.float32)]
    all_to_all x2 -> x0, waiting for transfers between devices: 18.3 us -> none  [the longest x1 9.47 us: body(): lax.all_to_all(placed.reshape((groups, local_count) + summed.shape[1:]).a...]
    all_to_all x2 -> x0, starting transfers between devices: 9.06 us -> none  [the longest x1 4.53 us: body(): lax.all_to_all(jnp.where(routing, encoded_bf[None], 0), 'dp', split_axis=...]
  transfers between devices with their start and end apart: 6 -> 0, of which waited for: 6 -> 0; matrix products, arithmetic and copies ran while one was open for 3% -> 0% of each run, Pallas kernels for 0% -> 0%
where the time goes in v1:
time: 173 us
  Pallas kernels  168 us (97%)
  local copies, waits for them, and re-layouts  3.87 us (2%)
    pallas_call x1, Pallas kernels, body(): pl.pallas_call(functools.partial(kernel, dims), out_shape=(jax.ShapeDtype...  168 us

profile of v1, /device:TPU:25, one launch (start us, length us, event | category | flops | bytes accessed | tf_op | source)
XLA Modules:
  0.0 172.7 jit_solution(2254475955234187362)
XLA Ops:
  0.6 0.7 convert_bitcast_fusion
  1.3 0.9 copy.10.mask
  2.2 167.5 %shard_map.95 = (bf16[4,128,1024]{2,1,0:T(8,128)(2,1)}, f32[2,64,512]{2,1,0:T(8,128)}) custom-call(s32[8]{0:T(128)} %counts.1, s32[8]{0:T(128)} %owner.1, f32[2,64,512]{2,1,0:T(8,128)} %encoded.1, bf16[1024,1024]{1,0:T(8,128)(2,1)} %bitcast.7, bf16[1024,1024]{1,0:T(8,128)(2,1)} %bitcast.8, bf16[4,128,1024]{2,1,0:T(8,128)(2,1)} %bitcast.10, ...), custom_call_target="tpu_custom_call" | custom-call | tf_op jit(solution)/shard_map/pallas_call | solution.py:486
  169.7 0.0 copy-start
  169.7 2.3 %copy.13 = bf16[1,4,128,1024]{3,2,1,0:T(8,128)(2,1)} copy(bf16[1,4,128,1024]{3,2,1,0:T(8,128)(2,1)} %bitcast.9) | data formatting | bytes 2097152
  172.0 0.0 copy-done
  172.0 0.7 copy.14
Async XLA Ops:
  169.7 2.3 %copy-start = (f32[2,64,512]{2,1,0:T(8,128)S(1)}, f32[2,64,512]{2,1,0:T(8,128)}, u32[]{:S(2)}) copy-start(f32[2,64,512]{2,1,0:T(8,128)} %get-tuple-element.9) | copy-start | bytes 786436

commit v2 on v1

v2 whole, which is shorter than its diff:
```python
import functools

import jax
import jax.numpy as jnp
from jax import lax
from jax.experimental import pallas as pl
from jax.experimental.pallas import tpu as pltpu
from jax.sharding import PartitionSpec as P

HEAD_DIM = 256
MESH = pl.DeviceIdType.MESH
F32 = jnp.float32
BF16 = jnp.bfloat16


def dot(left, right, left_dim, right_dim):
    return lax.dot_general(
        left, right, (((left_dim,), (right_dim,)), ((), ())), preferred_element_type=F32
    )


def kernel(
    dims,
    counts,
    owner,
    encoded,
    w_key,
    w_value,
    queries,
    grad_out,
    mask,
    attn_out,
    d_encoded,
    table,
    weights,
    enc_cast,
    enc_all,
    part,
    recv,
    send,
    own_grad,
    acc,
    d_send,
    d_pair,
    d_mid,
    d_recv,
    d_fin,
    d_arrived,
    w_sem,
    swap_send,
    swap_recv,
    self_sem,
    enc_send_sem,
    enc_pass_sem,
    enc_recv_sem,
    send_sem,
    recv_sem,
    pair_send_sem,
    pair_recv_sem,
    d_send_sem,
    d_recv_sem,
):
    sections, groups, cores = dims
    section = lax.axis_index("section")
    p = lax.axis_index("dp")
    core = lax.axis_index("mp")
    fold = sections // groups
    local_count, key_len, feat = encoded.shape
    dialogs = local_count * groups
    block_rows = local_count * key_len
    cap = queries.shape[0]
    heads = queries.shape[2] // HEAD_DIM
    per = local_count
    subs = groups
    pieces = heads * subs
    lag = 2 * subs
    others = cores - 1
    scale = HEAD_DIM ** (-0.5)

    swap_section, swap_p = p * fold + lax.rem(section, fold), section // fold
    stays = section // fold == p

    def region(s, m):
        rows = pl.multiple_of((s // fold) * block_rows, block_rows)
        cols = pl.multiple_of((lax.rem(s, fold) * cores + m) * feat, feat)
        return pl.ds(rows, block_rows), pl.ds(cols, feat)

    def remote(src, dst, out_sem, in_sem, device):
        return pltpu.make_async_remote_copy(
            src_ref=src,
            dst_ref=dst,
            send_sem=out_sem,
            recv_sem=in_sem,
            device_id=device,
            device_id_type=MESH,
        )

    barrier = pltpu.get_barrier_semaphore()

    def greet(s, z, m):
        pl.semaphore_signal(barrier, inc=1, device_id=(s, z, m), device_id_type=MESH)

    @pl.when(jnp.logical_not(stays))
    def _():
        greet(swap_section, swap_p, core)

    @pl.when(p > 0)
    def _():
        greet(section, p - 1, core)

    @pl.when(p < groups - 1)
    def _():
        greet(section, p + 1, core)

    @pl.loop(1, sections)
    def _(i):
        greet(lax.rem(section + i, sections), p, core)

    for j in range(1, cores):
        greet(section, p, lax.rem(core + j, cores))

    copies = []
    for h in range(heads):
        for kv, ref in enumerate((w_key, w_value)):
            copy = pltpu.make_async_copy(
                ref.at[:, pl.ds(h * HEAD_DIM, HEAD_DIM)],
                weights.at[2 * h + kv],
                w_sem.at[2 * h + kv],
            )
            copy.start()
            copies.append(copy)

    for a in range(local_count):
        enc_cast[pl.ds(a * key_len, key_len), :] = encoded[a].astype(BF16)

    pl.semaphore_wait(
        barrier,
        sections
        - 1
        + others
        + jnp.where(stays, 0, 1)
        + jnp.where(p > 0, 1, 0)
        + jnp.where(p < groups - 1, 1, 0),
    )

    m_rows, m_cols = region(section, core)
    mine_there = region(swap_section, core)

    def swap_copy():
        return remote(
            enc_cast,
            enc_all.at[mine_there[0], mine_there[1]],
            swap_send.at[0],
            swap_recv.at[0],
            (swap_section, swap_p, core),
        )

    @pl.when(stays)
    def _():
        copy = pltpu.make_async_copy(enc_cast, enc_all.at[m_rows, m_cols], self_sem.at[0])
        copy.start()
        copy.wait()

    @pl.when(jnp.logical_not(stays))
    def _():
        swap_copy().start()

    taken = jnp.int32(0)
    slot_dialog = [jnp.int32(0)] * cap
    slot_valid = [jnp.int32(0)] * cap
    slot_length = [jnp.int32(0)] * cap
    for d in range(dialogs):
        mine = (owner[d] == p).astype(jnp.int32)
        table[3 * cap + d] = jnp.where(mine == 1, jnp.minimum(taken, cap), cap)
        for c in range(cap):
            hit = mine * (taken == c).astype(jnp.int32)
            slot_dialog[c] = slot_dialog[c] + hit * d
            slot_valid[c] = slot_valid[c] + hit
            slot_length[c] = slot_length[c] + hit * counts[d]
        taken = taken + mine
    for c in range(cap):
        table[c] = slot_dialog[c]
        table[cap + c] = slot_valid[c]
        table[2 * cap + c] = slot_length[c]

    acc[...] = jnp.zeros_like(acc)
    own_grad[...] = jnp.zeros_like(own_grad)

    @pl.when(jnp.logical_not(stays))
    def _():
        remote(
            enc_cast,
            enc_all.at[m_rows, m_cols],
            swap_send.at[0],
            swap_recv.at[0],
            (swap_section, swap_p, core),
        ).wait_recv()

    def block_copy(s, out_sem, device):
        rows, cols = region(s[0], s[1])
        return remote(
            enc_all.at[rows, cols],
            enc_all.at[rows, cols],
            out_sem,
            enc_recv_sem.at[s[0] * cores + s[1]],
            device,
        )

    def spread(i):
        peer = lax.rem(section + i, sections)
        return block_copy((section, core), enc_send_sem.at[peer], (peer, p, core))

    def pass_on(s, j):
        return block_copy(
            (s, core),
            enc_pass_sem.at[s * others + j - 1],
            (section, p, lax.rem(core + j, cores)),
        )

    @pl.loop(1, sections)
    def _(i):
        spread(i).start()

    for j in range(1, cores):
        pass_on(section, j).start()

    for copy in copies:
        copy.wait()

    @pl.loop(1, sections)
    def _(i):
        s = lax.rem(section + sections - i, sections)
        block_copy((s, core), enc_send_sem.at[s], (s, p, core)).wait_recv()
        for j in range(1, cores):
            pass_on(s, j).start()

    @pl.loop(0, sections)
    def _(i):
        s = lax.rem(section + sections - i, sections)
        for j in range(1, cores):
            m = lax.rem(core + j, cores)
            block_copy((s, m), enc_send_sem.at[s], (section, p, m)).wait_recv()

    def hop(way, r):
        return remote(
            send.at[way, r],
            recv.at[way, r],
            send_sem.at[way, r],
            recv_sem.at[way, r],
            (section, p + 1 if way == 0 else p - 1, core),
        )

    def is_first(way):
        return p == 0 if way == 0 else p == groups - 1

    def is_last(way):
        return p == groups - 1 if way == 0 else p == 0

    def far(way):
        return p if way == 0 else groups - 1 - p

    def within(r, count):
        return jnp.logical_and(r >= 0, r < count)

    def ahead(way, r, i):
        d = lax.rem(r, subs) * per + i
        delta = owner[d] - p if way == 0 else p - owner[d]
        return jnp.full((key_len, HEAD_DIM), delta, jnp.int32)

    def own_rows(b, kv, i):
        return own_grad[b // subs, kv, table[3 * cap + lax.rem(b, subs) * per + i]].astype(F32)

    def project(h):
        for kv in range(2):
            product = dot(enc_all[...], weights[2 * h + kv], 1, 0).astype(BF16)
            part[pl.ds(h * subs, subs), kv] = product.reshape(subs, per, key_len, HEAD_DIM)

    def attend(h):
        cols = pl.ds(pl.multiple_of(h * HEAD_DIM, HEAD_DIM), HEAD_DIM)
        for c in range(cap):
            d = table[c]
            keep = table[cap + c].astype(F32)
            length = table[2 * cap + c]
            keys = (part[h * subs + d // per, 0, lax.rem(d, per)].astype(F32) * keep).astype(BF16)
            values = (
                part[h * subs + d // per, 1, lax.rem(d, per)].astype(F32) * keep
            ).astype(BF16)
            q = queries[c, :, cols]
            g = (grad_out[c, :, cols].astype(F32) * mask[c]).astype(BF16)
            scores = dot(q, keys, 1, 1) * scale
            ok = lax.broadcasted_iota(jnp.int32, scores.shape, 1) < length
            unnormed = jnp.where(ok, jnp.exp(scores), 0.0)
            attention = unnormed / (jnp.sum(unnormed, axis=1, keepdims=True) + (1.0 - keep))
            probs = attention.astype(BF16)
            attn_out[c, :, cols] = dot(probs, values, 1, 0).astype(BF16)
            own_grad[h, 1, c] = dot(probs, g, 0, 0).astype(BF16)
            grad_probs = dot(g, values, 1, 1)
            grad_scores = (
                attention
                * (grad_probs - jnp.sum(attention * grad_probs, axis=1, keepdims=True))
            ).astype(BF16)
            own_grad[h, 0, c] = (dot(grad_scores, q, 0, 0) * scale).astype(BF16)

    rounds = pieces + lag
    steps = rounds + groups - 1

    @pl.loop(0, steps)
    def _(t):
        @pl.when(jnp.logical_and(t < pieces, lax.rem(t, subs) == 0))
        def _():
            project(t // subs)

        for way in range(2):
            r = t - far(way)

            @pl.when(within(r, rounds))
            def _(way=way, r=r):
                fwd, bwd = jnp.minimum(r, pieces - 1), jnp.maximum(r - lag, 0)

                @pl.when(is_first(way))
                def _():
                    for kv in range(2):
                        for i in range(per):
                            send[way, r, kv, i] = jnp.where(
                                ahead(way, r, i) > 0,
                                part[fwd, kv, i].astype(F32),
                                own_rows(bwd, kv, i),
                            ).astype(BF16)

                @pl.when(jnp.logical_not(is_first(way)))
                def _():
                    hop(way, r).wait_recv()

                @pl.when(jnp.logical_not(jnp.logical_or(is_first(way), is_last(way))))
                def _():
                    for kv in range(2):
                        for i in range(per):
                            where_to = ahead(way, r, i)
                            came = recv[way, r, kv, i].astype(F32)
                            send[way, r, kv, i] = jnp.where(
                                where_to > 0,
                                came + part[fwd, kv, i].astype(F32),
                                jnp.where(where_to == 0, own_rows(bwd, kv, i), came),
                            ).astype(BF16)

                @pl.when(jnp.logical_not(is_last(way)))
                def _():
                    hop(way, r).start()

        whole = t - (groups - 1)

        @pl.when(within(whole, pieces))
        def _():
            @pl.when(p == 0)
            def _():
                part[whole] = (part[whole].astype(F32) + recv[1, whole].astype(F32)).astype(BF16)

            @pl.when(p == groups - 1)
            def _():
                part[whole] = (part[whole].astype(F32) + recv[0, whole].astype(F32)).astype(BF16)

            @pl.when(jnp.logical_and(p > 0, p < groups - 1))
            def _():
                part[whole] = (
                    part[whole].astype(F32)
                    + recv[0, whole].astype(F32)
                    + recv[1, whole].astype(F32)
                ).astype(BF16)

            @pl.when(lax.rem(whole, subs) == subs - 1)
            def _():
                attend(whole // subs)

        done = t - (groups - 1) - lag

        @pl.when(within(done, pieces))
        def _():
            r = done + lag

            def collect(below, above):
                for kv in range(2):
                    for i in range(per):
                        where_to = ahead(0, r, i)
                        rows = own_rows(done, kv, i)
                        if below:
                            rows = jnp.where(where_to < 0, recv[0, r, kv, i].astype(F32), rows)
                        if above:
                            rows = jnp.where(where_to > 0, recv[1, r, kv, i].astype(F32), rows)
                        part[done, kv, i] = rows.astype(BF16)

            @pl.when(p == 0)
            def _():
                collect(False, True)

            @pl.when(p == groups - 1)
            def _():
                collect(True, False)

            @pl.when(jnp.logical_and(p > 0, p < groups - 1))
            def _():
                collect(True, True)

            @pl.when(lax.rem(done, subs) == subs - 1)
            def _():
                h = done // subs
                for kv in range(2):
                    grads = part[pl.ds(h * subs, subs), kv].reshape(dialogs * key_len, HEAD_DIM)
                    acc[...] += dot(grads, weights[2 * h + kv], 1, 1)

    d_send[...] = acc[...].astype(BF16)

    def pair_copy(s, j):
        m = lax.rem(core + j, cores)
        rows, cols = region(s, m)
        k = s * others + j - 1
        return remote(
            d_send.at[rows, cols], d_pair.at[k], pair_send_sem.at[k], pair_recv_sem.at[k],
            (section, p, m),
        )

    def term_copy(s):
        return remote(
            d_mid.at[s], d_recv.at[section], d_send_sem.at[s], d_recv_sem.at[section],
            (s, p, core),
        )

    @pl.loop(1, sections + 1)
    def _(i):
        for j in range(1, cores):
            pair_copy(lax.rem(section + i, sections), j).start()

    def paired(s):
        rows, cols = region(s, core)
        total = acc[rows, cols]
        for j in range(1, cores):
            pair_copy(s, j).wait_recv()
            total = total + d_pair[s * others + j - 1].astype(F32)
        return total

    @pl.loop(1, sections)
    def _(i):
        s = lax.rem(section + i, sections)
        d_mid[s] = paired(s).astype(BF16)
        term_copy(s).start()

    acc[m_rows, m_cols] = paired(section)

    @pl.loop(1, sections)
    def _(i):
        s = lax.rem(section + sections - i, sections)
        remote(
            d_mid.at[s], d_recv.at[s], d_send_sem.at[s], d_recv_sem.at[s], (s, p, core)
        ).wait_recv()
        acc[m_rows, m_cols] += d_recv[s].astype(F32)

    d_fin[...] = acc[m_rows, m_cols].astype(BF16)

    def back_copy():
        return remote(
            d_fin, d_arrived, swap_send.at[1], swap_recv.at[1], (swap_section, swap_p, core)
        )

    @pl.when(stays)
    def _():
        for a in range(local_count):
            d_encoded[a] = d_fin[pl.ds(a * key_len, key_len), :].astype(F32)

    @pl.when(jnp.logical_not(stays))
    def _():
        back_copy().start()

    @pl.loop(0, rounds)
    def _(r):
        for way in range(2):

            @pl.when(jnp.logical_not(is_last(way)))
            def _(way=way):
                hop(way, r).wait_send()

    @pl.loop(1, sections)
    def _(i):
        spread(i).wait_send()
        term_copy(lax.rem(section + i, sections)).wait_send()

    @pl.loop(0, sections)
    def _(s):
        for j in range(1, cores):
            pass_on(s, j).wait_send()
            pair_copy(s, j).wait_send()

    @pl.when(jnp.logical_not(stays))
    def _():
        swap_copy().wait_send()
        back_copy().wait()
        for a in range(local_count):
            d_encoded[a] = d_arrived[pl.ds(a * key_len, key_len), :].astype(F32)


def body(dims, encoded, counts, owner, w_key, w_value, queries, grad_out, dec_mask):
    sections, groups, cores = dims
    local_count, key_len, feat = encoded.shape
    dialogs = local_count * groups
    cap, query_len, width = queries.shape[1:]
    model_rows = w_key.shape[1]
    heads = width // HEAD_DIM
    per = local_count
    pieces = heads * groups
    rounds = pieces + 2 * groups
    others = cores - 1
    block_rows = local_count * key_len
    item = (2, per, key_len, HEAD_DIM)
    dma = pltpu.SemaphoreType.DMA
    vmem = pl.BlockSpec(memory_space=pltpu.VMEM)
    smem = pl.BlockSpec(memory_space=pltpu.SMEM)
    hbm = pl.BlockSpec(memory_space=pl.ANY)
    mask = dec_mask.astype(F32)[:, :, None]
    attended, d_encoded = pl.pallas_call(
        functools.partial(kernel, dims),
        out_shape=(
            jax.ShapeDtypeStruct((cap, query_len, width), BF16),
            jax.ShapeDtypeStruct((local_count, key_len, feat), F32),
        ),
        in_specs=[smem, smem, vmem, hbm, hbm, vmem, vmem, vmem],
        out_specs=(vmem, vmem),
        scratch_shapes=[
            pltpu.SMEM((3 * cap + dialogs,), jnp.int32),
            pltpu.VMEM((2 * heads, model_rows, HEAD_DIM), BF16),
            pltpu.VMEM((block_rows, feat), BF16),
            pltpu.VMEM((dialogs * key_len, model_rows), BF16),
            pltpu.VMEM((pieces,) + item, BF16),
            pltpu.VMEM((2, rounds) + item, BF16),
            pltpu.VMEM((2, rounds) + item, BF16),
            pltpu.VMEM((heads, 2, cap + 1, key_len, HEAD_DIM), BF16),
            pltpu.VMEM((dialogs * key_len, model_rows), F32),
            pltpu.VMEM((dialogs * key_len, model_rows), BF16),
            pltpu.VMEM((sections * others, block_rows, feat), BF16),
            pltpu.VMEM((sections, block_rows, feat), BF16),
            pltpu.VMEM((sections, block_rows, feat), BF16),
            pltpu.VMEM((block_rows, feat), BF16),
            pltpu.VMEM((block_rows, feat), BF16),
            dma((2 * heads,)),
            dma((2,)),
            dma((2,)),
            dma((1,)),
            dma((sections,)),
            dma((sections * others,)),
            dma((sections * cores,)),
            dma((2, rounds)),
            dma((2, rounds)),
            dma((sections * others,)),
            dma((sections * others,)),
            dma((sections,)),
            dma((sections,)),
        ],
        compiler_params=pltpu.CompilerParams(
            collective_id=0, has_side_effects=True, vmem_limit_bytes=60 * 1024 * 1024
        ),
    )(counts, owner, encoded, w_key[0], w_value[0], queries[0], grad_out[0], mask)
    return (attended[None], d_encoded)


def solution(mesh):
    placed = (
        P("dp", None, ("section", "mp")),
        P(),
        P(),
        P("section", "dp", "mp"),
        P("section", "dp", "mp"),
        P("section", "dp", None, "mp"),
        P("section", "dp", None, "mp"),
        P("dp", None),
    )
    dims = tuple(mesh.shape[name] for name in ("section", "dp", "mp"))
    return jax.shard_map(
        functools.partial(body, dims),
        mesh=mesh,
        in_specs=placed,
        out_specs=(P("section", "dp", None, "mp"), P("dp", None, ("section", "mp"))),
        check_vma=False,
    )
```

time: 173 us -> 157 us (0.908); the launches traced: 173 us -> 155 us
  Pallas kernels: 168 us -> 149 us
    pallas_call x1, Pallas kernels: 168 us -> 149 us  [body(): pl.pallas_call(functools.partial(kernel, dims), out_shape=(jax.ShapeDtype...]
where the time goes in v2:
time: 157 us; the launch traced here: 155 us
  Pallas kernels  149 us (95%)
  local copies, waits for them, and re-layouts  3.87 us (2%)
    pallas_call x1, Pallas kernels, body(): pl.pallas_call(functools.partial(kernel, dims), out_shape=(jax.ShapeDtype...  149 us

profile of v2, /device:TPU:25, one launch (start us, length us, event | category | flops | bytes accessed | tf_op | source)
XLA Modules:
  0.0 154.5 jit_solution(11274280800490101439)
XLA Ops:
  0.6 0.7 convert_bitcast_fusion
  1.3 0.9 copy.10.mask
  2.2 149.3 %shard_map.95 = (bf16[4,128,1024]{2,1,0:T(8,128)(2,1)}, f32[2,64,512]{2,1,0:T(8,128)}) custom-call(s32[8]{0:T(128)} %counts.1, s32[8]{0:T(128)} %owner.1, f32[2,64,512]{2,1,0:T(8,128)} %encoded.1, bf16[1024,1024]{1,0:T(8,128)(2,1)} %bitcast.7, bf16[1024,1024]{1,0:T(8,128)(2,1)} %bitcast.8, bf16[4,128,1024]{2,1,0:T(8,128)(2,1)} %bitcast.10, ...), custom_call_target="tpu_custom_call" | custom-call | tf_op jit(solution)/shard_map/pallas_call | solution.py:517
  151.5 0.0 copy-start
  151.5 2.3 %copy.13 = bf16[1,4,128,1024]{3,2,1,0:T(8,128)(2,1)} copy(bf16[1,4,128,1024]{3,2,1,0:T(8,128)(2,1)} %bitcast.9) | data formatting | bytes 2097152
  153.8 0.0 copy-done
  153.8 0.7 copy.14
Async XLA Ops:
  151.5 2.3 %copy-start = (f32[2,64,512]{2,1,0:T(8,128)S(1)}, f32[2,64,512]{2,1,0:T(8,128)}, u32[]{:S(2)}) copy-start(f32[2,64,512]{2,1,0:T(8,128)} %get-tuple-element.9) | copy-start | bytes 786436

commit v3 on v2

--- a/solution.py
+++ b/solution.py
@@ -11,6 +11,14 @@
 MESH = pl.DeviceIdType.MESH
 F32 = jnp.float32
 BF16 = jnp.bfloat16
+
+
+def skew(hops):
+    return (5 * hops + 1) // 3
+
+
+def lag_of(groups):
+    return pl.cdiv(groups - 1 + skew(groups - 1), groups) * groups
 
 
 def dot(left, right, left_dim, right_dim):
@@ -73,7 +81,8 @@
     per = local_count
     subs = groups
     pieces = heads * subs
-    lag = 2 * subs
+    lag = lag_of(groups)
+    late = skew(groups - 1)
     others = cores - 1
     scale = HEAD_DIM ** (-0.5)
 
@@ -257,7 +266,7 @@
         return p == groups - 1 if way == 0 else p == 0
 
     def far(way):
-        return p if way == 0 else groups - 1 - p
+        return skew(p if way == 0 else groups - 1 - p)
 
     def within(r, count):
         return jnp.logical_and(r >= 0, r < count)
@@ -302,7 +311,7 @@
             own_grad[h, 0, c] = (dot(grad_scores, q, 0, 0) * scale).astype(BF16)
 
     rounds = pieces + lag
-    steps = rounds + groups - 1
+    steps = rounds + late
 
     @pl.loop(0, steps)
     def _(t):
@@ -317,22 +326,12 @@
             def _(way=way, r=r):
                 fwd, bwd = jnp.minimum(r, pieces - 1), jnp.maximum(r - lag, 0)
 
-                @pl.when(is_first(way))
-                def _():
-                    for kv in range(2):
-                        for i in range(per):
-                            send[way, r, kv, i] = jnp.where(
-                                ahead(way, r, i) > 0,
-                                part[fwd, kv, i].astype(F32),
-                                own_rows(bwd, kv, i),
-                            ).astype(BF16)
-
                 @pl.when(jnp.logical_not(is_first(way)))
                 def _():
                     hop(way, r).wait_recv()
 
                 @pl.when(jnp.logical_not(jnp.logical_or(is_first(way), is_last(way))))
-                def _():
+                def _(fwd=fwd, bwd=bwd):
                     for kv in range(2):
                         for i in range(per):
                             where_to = ahead(way, r, i)
@@ -343,11 +342,9 @@
                                 jnp.where(where_to == 0, own_rows(bwd, kv, i), came),
                             ).astype(BF16)
 
-                @pl.when(jnp.logical_not(is_last(way)))
-                def _():
                     hop(way, r).start()
 
-        whole = t - (groups - 1)
+        whole = t - late
 
         @pl.when(within(whole, pieces))
         def _():
@@ -371,7 +368,21 @@
             def _():
                 attend(whole // subs)
 
-        done = t - (groups - 1) - lag
+        for way in range(2):
+
+            @pl.when(jnp.logical_and(is_first(way), t < rounds))
+            def _(way=way):
+                fwd, bwd = jnp.minimum(t, pieces - 1), jnp.maximum(t - lag, 0)
+                for kv in range(2):
+                    for i in range(per):
+                        send[way, t, kv, i] = jnp.where(
+                            ahead(way, t, i) > 0,
+                            part[fwd, kv, i].astype(F32),
+                            own_rows(bwd, kv, i),
+                        ).astype(BF16)
+                hop(way, t).start()
+
+        done = t - late - lag
 
         @pl.when(within(done, pieces))
         def _():
@@ -505,7 +516,7 @@
     heads = width // HEAD_DIM
     per = local_count
     pieces = heads * groups
-    rounds = pieces + 2 * groups
+    rounds = pieces + lag_of(groups)
     others = cores - 1
     block_rows = local_count * key_len
     item = (2, per, key_len, HEAD_DIM)

time: 157 us -> 145 us (0.924)
  Pallas kernels: 149 us -> 137 us
    pallas_call x1, Pallas kernels: 149 us -> 137 us  [body(): pl.pallas_call(functools.partial(kernel, dims), out_shape=(jax.ShapeDtype...]
where the time goes in v3:
time: 145 us; the launch traced here: 143 us
  Pallas kernels  137 us (94%)
  local copies, waits for them, and re-layouts  3.87 us (3%)
    pallas_call x1, Pallas kernels, body(): pl.pallas_call(functools.partial(kernel, dims), out_shape=(jax.ShapeDtype...  137 us
    unnamed x4, local copies, waits for them, and re-layouts  3.01 us

profile of v3, /device:TPU:25, one launch (start us, length us, event | category | flops | bytes accessed | tf_op | source)
XLA Modules:
  0.0 142.5 jit_solution(5375854113679820428)
XLA Ops:
  0.6 0.7 convert_bitcast_fusion
  1.3 0.9 copy.10.mask
  2.2 137.3 %shard_map.95 = (bf16[4,128,1024]{2,1,0:T(8,128)(2,1)}, f32[2,64,512]{2,1,0:T(8,128)}) custom-call(s32[8]{0:T(128)} %counts.1, s32[8]{0:T(128)} %owner.1, f32[2,64,512]{2,1,0:T(8,128)} %encoded.1, bf16[1024,1024]{1,0:T(8,128)(2,1)} %bitcast.7, bf16[1024,1024]{1,0:T(8,128)(2,1)} %bitcast.8, bf16[4,128,1024]{2,1,0:T(8,128)(2,1)} %bitcast.10, ...), custom_call_target="tpu_custom_call" | custom-call | tf_op jit(solution)/shard_map/pallas_call | solution.py:528
  139.5 0.0 copy-start
  139.5 2.3 %copy.13 = bf16[1,4,128,1024]{3,2,1,0:T(8,128)(2,1)} copy(bf16[1,4,128,1024]{3,2,1,0:T(8,128)(2,1)} %bitcast.9) | data formatting | bytes 2097152
  141.8 0.0 copy-done
  141.8 0.7 copy.14
Async XLA Ops:
  139.5 2.3 %copy-start = (f32[2,64,512]{2,1,0:T(8,128)S(1)}, f32[2,64,512]{2,1,0:T(8,128)}, u32[]{:S(2)}) copy-start(f32[2,64,512]{2,1,0:T(8,128)} %get-tuple-element.9) | copy-start | bytes 786436

commit v4 on v3

--- a/solution.py
+++ b/solution.py
@@ -14,7 +14,7 @@
 
 
 def skew(hops):
-    return (5 * hops + 1) // 3
+    return (5 * hops + 2) // 3
 
 
 def lag_of(groups):

time: 145 us -> 141 us (0.972); the launches traced: 143 us -> 141 us
  Pallas kernels: 137 us -> 135 us
    pallas_call x1, Pallas kernels: 137 us -> 135 us  [body(): pl.pallas_call(functools.partial(kernel, dims), out_shape=(jax.ShapeDtype...]
where the time goes in v4:
time: 141 us
  Pallas kernels  135 us (96%)
  local copies, waits for them, and re-layouts  3.87 us (3%)
    pallas_call x1, Pallas kernels, body(): pl.pallas_call(functools.partial(kernel, dims), out_shape=(jax.ShapeDtype...  135 us
    unnamed x4, local copies, waits for them, and re-layouts  3.01 us

profile of v4, /device:TPU:25, one launch (start us, length us, event | category | flops | bytes accessed | tf_op | source)
XLA Modules:
  0.0 140.5 jit_solution(2055923801177537904)
XLA Ops:
  0.6 0.7 convert_bitcast_fusion
  1.3 0.9 copy.10.mask
  2.2 135.3 %shard_map.95 = (bf16[4,128,1024]{2,1,0:T(8,128)(2,1)}, f32[2,64,512]{2,1,0:T(8,128)}) custom-call(s32[8]{0:T(128)} %counts.1, s32[8]{0:T(128)} %owner.1, f32[2,64,512]{2,1,0:T(8,128)} %encoded.1, bf16[1024,1024]{1,0:T(8,128)(2,1)} %bitcast.7, bf16[1024,1024]{1,0:T(8,128)(2,1)} %bitcast.8, bf16[4,128,1024]{2,1,0:T(8,128)(2,1)} %bitcast.10, ...), custom_call_target="tpu_custom_call" | custom-call | tf_op jit(solution)/shard_map/pallas_call | solution.py:528
  137.5 0.0 copy-start
  137.5 2.3 %copy.13 = bf16[1,4,128,1024]{3,2,1,0:T(8,128)(2,1)} copy(bf16[1,4,128,1024]{3,2,1,0:T(8,128)(2,1)} %bitcast.9) | data formatting | bytes 2097152
  139.8 0.0 copy-done
  139.8 0.7 copy.14
Async XLA Ops:
  137.5 2.3 %copy-start = (f32[2,64,512]{2,1,0:T(8,128)S(1)}, f32[2,64,512]{2,1,0:T(8,128)}, u32[]{:S(2)}) copy-start(f32[2,64,512]{2,1,0:T(8,128)} %get-tuple-element.9) | copy-start | bytes 786436
